TPU v7x, 512 devices: a whole 4x8x8 slice. The times are simulated.
512 devices in a mesh: interval: 8 (over y), seq: 8 (over x, core), head: 8 (over z).
Axes of the slice: x: 4, y: 8, z: 8, core: 2. Of those that a mesh axis runs over, the one named last changes fastest.
Arguments:
- hidden_in: bfloat16 [8, 2048, 1536], P('interval', 'seq'), may hold values from -6 to 6
- ctx_grad: bfloat16 [8, 2048, 1536], P('interval', 'seq', 'head'), may hold values from -6 to 6
- w_query: bfloat16 [1536, 1536], P('head'), may hold values from -0.15625 to 0.15625
- w_key: bfloat16 [1536, 1536], P('head'), may hold values from -0.15625 to 0.15625
- w_value: bfloat16 [1536, 1536], P('head'), may hold values from -0.15625 to 0.15625
- w_junction: bfloat16 [1536, 128], replicated, may hold values from -0.15625 to 0.15625
- donor_pos: int32 [8, 8, 8, 64], P('interval', 'seq', None, 'head'), may hold values from 0 to 255
- acceptor_pos: int32 [8, 8, 8, 64], P('interval', 'seq', None, 'head'), may hold values from 0 to 255
- junction_counts: int32 [8, 8, 8], P('interval', 'seq'), may hold values from 16 to 64, as said below
- pred_grad: float32 [8, 8, 8, 64], P('interval', 'seq', None, 'head'), may hold values from -6 to 6
Outputs:
- grad_input: bfloat16 [8, 2048, 1536], P('interval', 'seq', 'head')
- grad_query: bfloat16 [1536, 1536], P('head')
- grad_key: bfloat16 [1536, 1536], P('head')
- grad_value: bfloat16 [1536, 1536], P('head')
Inputs may be any that keep to these rules, and one draw needn't show every extreme that they name: `junction_counts`: slots at or past a bucket's count are empty. In each interval one acceptor shard, drawn from the seed, has 64 live slots from every donor shard; every other bucket has 16 to 32.
All inputs are finite; a program needn't handle non-finite values.
Results may differ from a plain program's by a relative error of at most 0.022.
Values may be sent and summed in bfloat16 or wider, within the bound.
No kernel may reach another device: no remote copies, remote signals or barrier semaphores. Data moves between devices by JAX's collectives and lax.ppermute only.
A program may use at most 64 MiB of HBM per device.

v0:
```python
import jax
import jax.numpy as jnp
from jax import lax
from jax.sharding import PartitionSpec as P

HD = 192
PJ = 128


def on_device(
    hidden_in,
    ctx_grad,
    w_query,
    w_key,
    w_value,
    w_junction,
    donor_pos,
    acceptor_pos,
    junction_counts,
    pred_grad,
):
    hidden = hidden_in[0]
    local_len = hidden.shape[0]
    shard_count = lax.axis_size("seq")
    total_len = local_len * shard_count
    heads_dev = w_query.shape[0] // HD
    softmax_scale = HD ** (-0.5)
    pair_scale = PJ ** (-0.5)
    queries = jnp.einsum("td,cd->tc", hidden, w_query, preferred_element_type=jnp.float32).astype(
        jnp.bfloat16
    )
    key_rows = jnp.einsum("td,cd->tc", hidden, w_key, preferred_element_type=jnp.float32).astype(
        jnp.bfloat16
    )
    value_rows = jnp.einsum(
        "td,cd->tc", hidden, w_value, preferred_element_type=jnp.float32
    ).astype(jnp.bfloat16)
    features = jnp.dot(hidden, w_junction, preferred_element_type=jnp.float32).astype(jnp.bfloat16)
    all_keys, all_values, all_features = (
        lax.all_gather(key_rows, "seq", axis=0, tiled=True),
        lax.all_gather(value_rows, "seq", axis=0, tiled=True),
        lax.all_gather(features, "seq", axis=0, tiled=True),
    )
    query_heads = queries.reshape(local_len, heads_dev, HD)
    grad_heads = ctx_grad[0].reshape(local_len, heads_dev, HD)
    key_heads = all_keys.reshape(total_len, heads_dev, HD)
    value_heads = all_values.reshape(total_len, heads_dev, HD)
    scores = (
        jnp.einsum("qhd,khd->hqk", query_heads, key_heads, preferred_element_type=jnp.float32)
        * softmax_scale
    )
    row_max = jnp.max(scores, axis=-1, keepdims=True)
    expd = jnp.exp(scores - row_max)
    probs = expd / jnp.sum(expd, axis=-1, keepdims=True)
    dprobs = jnp.einsum("qhd,khd->hqk", grad_heads, value_heads, preferred_element_type=jnp.float32)
    row_delta = jnp.sum(probs * dprobs, axis=-1, keepdims=True)
    dscores = probs * (dprobs - row_delta)
    probs_b = probs.astype(jnp.bfloat16)
    dscores_b = dscores.astype(jnp.bfloat16)
    query_grad = (
        (
            jnp.einsum("hqk,khd->qhd", dscores_b, key_heads, preferred_element_type=jnp.float32)
            * softmax_scale
        )
        .astype(jnp.bfloat16)
        .reshape(local_len, heads_dev * HD)
    )
    key_term = (
        jnp.einsum("hqk,qhd->khd", dscores_b, query_heads, preferred_element_type=jnp.float32)
        * softmax_scale
    ).reshape(total_len, heads_dev * HD)
    value_term = jnp.einsum(
        "hqk,qhd->khd", probs_b, grad_heads, preferred_element_type=jnp.float32
    ).reshape(total_len, heads_dev * HD)
    key_sum, value_sum = (
        lax.psum_scatter(
            key_term.astype(jnp.bfloat16), "seq", scatter_dimension=0, tiled=True
        ).astype(jnp.float32),
        lax.psum_scatter(
            value_term.astype(jnp.bfloat16), "seq", scatter_dimension=0, tiled=True
        ).astype(jnp.float32),
    )
    key_grad = key_sum.astype(jnp.bfloat16)
    value_grad = value_sum.astype(jnp.bfloat16)
    donor_idx = donor_pos[0, 0]
    accept_idx = acceptor_pos[0, 0]
    slot_dev = donor_idx.shape[1]
    slot_ids = lax.axis_index("head") * slot_dev + jnp.arange(slot_dev, dtype=jnp.int32)
    live_slots = slot_ids[None, :] < junction_counts[0, 0][:, None]
    donor_feat = features[donor_idx].astype(jnp.float32)
    accept_glob = jnp.arange(shard_count, dtype=jnp.int32)[:, None] * local_len + accept_idx
    accept_rows = all_features[accept_glob]
    accept_feat = accept_rows.astype(jnp.float32)
    pair_score = jnp.sum(donor_feat * accept_feat, axis=-1) * pair_scale
    slot_grad = (
        jnp.where(live_slots, pred_grad[0, 0] * jax.nn.sigmoid(pair_score), 0.0) * pair_scale
    )
    donor_term = slot_grad[..., None] * accept_feat
    accept_term = slot_grad[..., None] * donor_feat
    pair_width = features.shape[1]
    grad_feat = (
        jnp.zeros((local_len, pair_width), jnp.float32)
        .at[donor_idx.reshape(-1)]
        .add(donor_term.reshape(-1, pair_width))
    )
    spread_term = (
        jnp.zeros((total_len, pair_width), jnp.float32)
        .at[accept_glob.reshape(-1)]
        .add(accept_term.reshape(-1, pair_width))
    )
    grad_feat = grad_feat + lax.psum_scatter(
        spread_term.astype(jnp.bfloat16), "seq", scatter_dimension=0, tiled=True
    ).astype(jnp.float32)
    grad_feat_b = grad_feat.astype(jnp.bfloat16)
    input_term = jnp.einsum("tc,cd->td", query_grad, w_query, preferred_element_type=jnp.float32)
    input_term = input_term + jnp.einsum(
        "tc,cd->td", key_grad, w_key, preferred_element_type=jnp.float32
    )
    input_term = input_term + jnp.einsum(
        "tc,cd->td", value_grad, w_value, preferred_element_type=jnp.float32
    )
    input_term = input_term + jnp.einsum(
        "tp,dp->td", grad_feat_b, w_junction, preferred_element_type=jnp.float32
    )
    grad_input = lax.psum_scatter(
        input_term.astype(jnp.bfloat16), "head", scatter_dimension=1, tiled=True
    )
    key_wterm = jnp.einsum("tc,td->cd", key_grad, hidden, preferred_element_type=jnp.float32)
    value_wterm = jnp.einsum("tc,td->cd", value_grad, hidden, preferred_element_type=jnp.float32)
    query_wterm = jnp.einsum("tc,td->cd", query_grad, hidden, preferred_element_type=jnp.float32)
    query_wsum, key_wsum, value_wsum = lax.psum(
        (query_wterm, key_wterm, value_wterm), ("interval", "seq")
    )
    return (
        grad_input[None],
        query_wsum.astype(jnp.bfloat16),
        key_wsum.astype(jnp.bfloat16),
        value_wsum.astype(jnp.bfloat16),
    )


def solution(mesh):
    placed = (
        P("interval", "seq", None),
        P("interval", "seq", "head"),
        P("head", None),
        P("head", None),
        P("head", None),
        P(),
        P("interval", "seq", None, "head"),
        P("interval", "seq", None, "head"),
        P("interval", "seq", None),
        P("interval", "seq", None, "head"),
    )
    return jax.shard_map(
        on_device,
        mesh=mesh,
        in_specs=placed,
        out_specs=(P("interval", "seq", "head"), P("head", None), P("head", None), P("head", None)),
        check_vma=False,
    )
```

profile of v0, /device:TPU:64, one launch (start us, length us, event | category | flops | bytes accessed | tf_op | source)
XLA Modules:
  0.0 447.5 jit_solution(17675293737374444175)
XLA Ops:
  7.2 0.0 copy-start
  7.2 0.0 reduce-scatter.9.cloned.1.call-start
  7.2 0.8 squeeze.15
  8.1 0.8 compare_select_fusion
  8.8 0.1 add.132
  8.9 0.1 add.133
  9.0 0.7 compare_select_fusion.1
  9.7 0.1 reshape.274
  9.8 1.3 convolution_convert_fusion.4
  11.1 0.0 copy-start.4
  11.1 13.6 %all_gather.11 = bf16[2048,128]{1,0:T(8,128)(2,1)S(1)} all-gather(bf16[256,128]{1,0:T(8,128)(2,1)S(1)} %convolution_convert_fusion.4), channel_id=1, replica_groups=mesh['interval'=8,'seq'=8,'head'=8] {'seq'}, dimensions={0}, use_global_device_ids=true | all-gather | bytes 589824 | tf_op jit(solution)/shard_map/all_gather | solution.py:42
  24.7 0.6 gather_fusion
  25.4 0.8 squeeze.16
  26.1 0.1 reshape.282
  26.2 0.1 lt.65
  26.3 0.7 lt.67
  27.1 0.1 lt.68
  27.1 0.6 gather_fusion.1
  27.8 0.1 fusion.23
  27.9 1.1 scatter_custom_fusion
  29.1 0.0 copy-start.3
  29.1 0.8 convert_element_type.105
  29.9 0.0 reduce-scatter.9.cloned.1.call-update
  29.9 0.0 reduce-scatter.5.cloned.1.call-start
  30.0 0.4 convolution_convert_fusion.3
  30.4 13.4 %all_gather.9 = bf16[2048,192]{0,1:T(8,128)(2,1)S(1)} all-gather(bf16[256,192]{0,1:T(8,128)(2,1)S(1)} %convolution_convert_fusion.3), channel_id=1, replica_groups=mesh['interval'=8,'seq'=8,'head'=8] {'seq'}, dimensions={0}, use_global_device_ids=true | all-gather | bytes 884736 | tf_op jit(solution)/shard_map/all_gather | solution.py:40
  43.8 0.4 convolution_convert_fusion.2
  44.2 0.0 copy-done.6
  44.2 0.4 convolution_convert_fusion.1
  44.6 14.2 %all_gather.10 = bf16[2048,192]{1,0:T(8,128)(2,1)S(1)} all-gather(bf16[256,192]{1,0:T(8,128)(2,1)S(1)} %convolution_convert_fusion.1), channel_id=1, replica_groups=mesh['interval'=8,'seq'=8,'head'=8] {'seq'}, dimensions={0}, use_global_device_ids=true | all-gather | bytes 884736 | tf_op jit(solution)/shard_map/all_gather | solution.py:41
  58.8 0.5 fusion.31
  59.3 0.4 fusion.4
  59.8 0.0 copy-done.11
  59.8 0.7 multiply_reduce_fusion
  60.5 0.6 multiply_convert_fusion
  61.1 1.0 copy-done.1
  62.1 1.3 fusion.2
  63.4 0.0 reduce-scatter.5.cloned.1.call-update
  63.5 0.0 copy-start.10
  63.5 0.0 reduce-scatter.7.cloned.1.call-start
  63.5 2.4 convolution_convert_fusion
  65.9 0.0 reduce-scatter.7.cloned.1.call-update
  66.0 0.0 reduce-scatter.11.cloned.1.call-start
  66.0 0.0 copy-done.10
  66.0 0.1 reshape_squeeze.4
  66.1 2.0 fusion.6
  68.1 0.5 fusion.32
  68.6 0.0 copy-start.7
  68.6 1.5 reduce-scatter.9.cloned.1.call-done
  70.1 0.8 convert_element_type.106
  70.9 1.1 scatter_custom_fusion.1
  72.0 37.1 %reduce-scatter.5.cloned.1.call-done = bf16[256,192]{0,1:T(8,128)(2,1)} async-done(((bf16[2048,192]{0,1:T(8,128)(2,1)}), bf16[256,192]{0,1:T(8,128)(2,1)}) %reduce-scatter.5.cloned.1.call-update) | async-done | bytes 98320 | tf_op jit(solution)/shard_map/reduce_scatter | solution.py:76
  109.1 2.7 convolution_add_fusion.2
  111.8 35.7 %reduce-scatter.7.cloned.1.call-done = bf16[256,192]{0,1:T(8,128)(2,1)} async-done(((bf16[2048,192]{0,1:T(8,128)(2,1)}), bf16[256,192]{0,1:T(8,128)(2,1)}) %reduce-scatter.7.cloned.1.call-update) | async-done | bytes 98320 | tf_op jit(solution)/shard_map/reduce_scatter | solution.py:79
  147.5 0.0 copy-done.7
  147.5 1.9 convolution_add_fusion.1
  149.4 0.0 copy-done.5
  149.5 1.3 fusion
  150.7 0.0 reduce-scatter.11.cloned.1.call-update
  150.8 0.3 fusion.12
  151.1 0.5 copy-done.8
  151.6 0.3 fusion.10
  152.0 1.3 fusion.8
  153.3 287.6 %all-reduce.2 = (bf16[192,1536]{1,0:T(8,128)(2,1)}, bf16[192,1536]{1,0:T(8,128)(2,1)}, bf16[192,1536]{1,0:T(8,128)(2,1)}) all-reduce(f32[192,1536]{1,0:T(8,128)S(1)} %fusion.12, f32[192,1536]{1,0:T(8,128)S(1)} %fusion.10, f32[192,1536]{1,0:T(8,128)} %fusion.8), channel_id=1, replica_groups=mesh['interval'=8,'seq'=8,'head'=8] {'interval','seq'}, use_global_device_ids=true, to_apply=%region_10.11 | all-reduce | flops 884736 | bytes 5308416 | tf_op jit(solution)/shard_map/psum | solution.py:131
  (21 shorter events, 0.1 us)
Async XLA Ops:
  7.2 2.6 copy-start
  7.2 62.9 %reduce-scatter.9.cloned.1.call-start = ((), (), s32[]{:S(2)}) async-start(), calls=%async_computation.6 | async-start | bytes 589824 | tf_op jit(solution)/shard_map/reduce_scatter | solution.py:111
  11.1 18.9 %copy-start.4 = (bf16[192,1536]{1,0:T(8,128)(2,1)S(1)}, bf16[192,1536]{1,0:T(8,128)(2,1)}, u32[]{:S(2)}) copy-start(bf16[192,1536]{1,0:T(8,128)(2,1)} %param.13) | copy-start | bytes 1769476
  29.1 14.7 %copy-start.3 = (bf16[192,1536]{1,0:T(8,128)(2,1)S(1)}, bf16[192,1536]{1,0:T(8,128)(2,1)}, u32[]{:S(2)}) copy-start(bf16[192,1536]{1,0:T(8,128)(2,1)} %param.12) | copy-start | bytes 1769476
  29.9 14.3 %copy-start.6 = (bf16[192,1536]{1,0:T(8,128)(2,1)S(1)}, bf16[192,1536]{1,0:T(8,128)(2,1)}, u32[]{:S(2)}) copy-start(bf16[192,1536]{1,0:T(8,128)(2,1)} %param.14) | copy-start | bytes 1769476
  29.9 79.1 %reduce-scatter.5.cloned.1.call-start = ((), (), s32[]{:S(2)}) async-start(), calls=%async_computation.4 | async-start | bytes 884736 | tf_op jit(solution)/shard_map/reduce_scatter | solution.py:76
  43.8 15.0 %copy-start.2 = (bf16[2048,192]{0,1:T(8,128)(2,1)}, bf16[2048,192]{0,1:T(8,128)(2,1)S(1)}, u32[]{:S(2)}) copy-start(bf16[2048,192]{0,1:T(8,128)(2,1)S(1)} %all_gather.9) | copy-start | bytes 2359300
  58.8 1.0 copy-start.11
  61.1 1.0 copy-start.1
  63.5 2.6 copy-start.10
  63.5 84.0 %reduce-scatter.7.cloned.1.call-start = ((), (), s32[]{:S(2)}) async-start(), calls=%async_computation.5 | async-start | bytes 884736 | tf_op jit(solution)/shard_map/reduce_scatter | solution.py:79
  66.0 375.0 %reduce-scatter.11.cloned.1.call-start = ((), (), s32[]{:S(2)}) async-start(), calls=%async_computation.7 | async-start | bytes 884736 | tf_op jit(solution)/shard_map/reduce_scatter | solution.py:125
  68.6 79.0 %copy-start.7 = (bf16[192,1536]{1,0:T(8,128)(2,1)S(1)}, bf16[192,1536]{1,0:T(8,128)(2,1)}, u32[]{:S(2)}) copy-start(bf16[192,1536]{1,0:T(8,128)(2,1)} %param.14) | copy-start | bytes 1769476
  111.8 37.6 %copy-start.5 = (bf16[1536,128]{1,0:T(8,128)(2,1)S(1)}, bf16[1536,128]{1,0:T(8,128)(2,1)}, u32[]{:S(2)}) copy-start(bf16[1536,128]{1,0:T(8,128)(2,1)} %param.15) | copy-start | bytes 1179652
  150.7 0.9 copy-start.8
  150.8 1.2 copy-start.9
Sparse Core Ops, SparseCore 0:
  30.1 39.9 reduce-scatter.8
  73.1 35.9 reduce-scatter.4
  111.9 35.5 reduce-scatter.6
  151.0 39.1 reduce-scatter.10
where the time goes:
time: 448 us; the launch traced here: 447 us
  blocking collectives  329 us (73%)
  waiting for transfers between devices  74.4 us (17%)
  matrix products  17.9 us (4%)
  between operations  14 us (3%)
  other arithmetic  6.55 us (1%)
  local copies, waits for them, and re-layouts  5.71 us (1%)
    psum x1, blocking collectives, on_device(): lax.psum((query_wterm, key_wterm, value_wterm), ('interval', 'seq'))  288 us
    reduce_scatter x1, waiting for transfers between devices, on_device(): lax.psum_scatter(key_term.astype(jnp.bfloat16), 'seq', scatter_dimension=...  37.1 us
    reduce_scatter x1, waiting for transfers between devices, on_device(): lax.psum_scatter(value_term.astype(jnp.bfloat16), 'seq', scatter_dimensio...  35.7 us
    all_gather x1, blocking collectives, on_device(): lax.all_gather(value_rows, 'seq', axis=0, tiled=True)  14.2 us
    all_gather x1, blocking collectives, on_device(): lax.all_gather(features, 'seq', axis=0, tiled=True)  13.6 us
    all_gather x1, blocking collectives, on_device(): lax.all_gather(key_rows, 'seq', axis=0, tiled=True)  13.4 us
  transfers between devices with their start and end apart: 4, of which 3 were waited for; matrix products, arithmetic and copies ran while one was open for 4% of the time, Pallas kernels for 0%

commit v1 on v0

--- a/solution.py
+++ b/solution.py
@@ -1,3 +1,4 @@
+import functools
 import jax
 import jax.numpy as jnp
 from jax import lax
@@ -5,6 +6,14 @@
 
 HD = 192
 PJ = 128
+
+
+def pack_view_now(patch, group_axis, mesh_name):
+    lower = lax.psum(patch, group_axis)
+    return lax.psum(lower, mesh_name)
+
+
+feed_indices = functools.partial(pack_view_now, group_axis="interval", mesh_name="seq")
 
 
 def on_device(
@@ -128,9 +137,7 @@
     key_wterm = jnp.einsum("tc,td->cd", key_grad, hidden, preferred_element_type=jnp.float32)
     value_wterm = jnp.einsum("tc,td->cd", value_grad, hidden, preferred_element_type=jnp.float32)
     query_wterm = jnp.einsum("tc,td->cd", query_grad, hidden, preferred_element_type=jnp.float32)
-    query_wsum, key_wsum, value_wsum = lax.psum(
-        (query_wterm, key_wterm, value_wterm), ("interval", "seq")
-    )
+    query_wsum, key_wsum, value_wsum = feed_indices((query_wterm, key_wterm, value_wterm))
     return (
         grad_input[None],
         query_wsum.astype(jnp.bfloat16),

time: 448 us -> 331 us (0.74)
  the two profiles are of different devices: /device:TPU:64 before, /device:TPU:24 now
where the time goes in v1:
time: 331 us
  waiting for transfers between devices  182 us (55%)
  blocking collectives  100 us (30%)
  matrix products  20.5 us (6%)
  between operations  14.1 us (4%)
  other arithmetic  7.82 us (2%)
  local copies, waits for them, and re-layouts  5.88 us (2%)
    psum x1, waiting for transfers between devices, pack_view_now(): lower = lax.psum(patch, group_axis)  98.1 us
    psum x1, blocking collectives, pack_view_now(): return lax.psum(lower, mesh_name)  58.6 us
    reduce_scatter x1, waiting for transfers between devices, on_device(): lax.psum_scatter(value_term.astype(jnp.bfloat16), 'seq', scatter_dimensio...  36.5 us
    reduce_scatter x1, waiting for transfers between devices, on_device(): lax.psum_scatter(spread_term.astype(jnp.bfloat16), 'seq', scatter_dimensi...  34.3 us
    all_gather x1, blocking collectives, on_device(): lax.all_gather(features, 'seq', axis=0, tiled=True)  14.2 us
    all_gather x1, blocking collectives, on_device(): lax.all_gather(key_rows, 'seq', axis=0, tiled=True)  13.7 us
    all_gather x1, blocking collectives, on_device(): lax.all_gather(value_rows, 'seq', axis=0, tiled=True)  13.7 us
    reduce_scatter x1, waiting for transfers between devices, on_device(): lax.psum_scatter(key_term.astype(jnp.bfloat16), 'seq', scatter_dimension=...  12.8 us
  transfers between devices with their start and end apart: 5, of which 4 were waited for; matrix products, arithmetic and copies ran while one was open for 8% of the time, Pallas kernels for 0%

profile of v1, /device:TPU:24, one launch (start us, length us, event | category | flops | bytes accessed | tf_op | source)
XLA Modules:
  0.0 330.5 jit_solution(18122075059134062253)
XLA Ops:
  7.2 0.0 copy-start
  7.2 0.0 copy-start.9
  7.2 0.0 reduce-scatter.5.cloned.1.call-start
  7.2 1.1 copy-done
  8.3 1.5 convolution_convert_fusion.3
  9.8 13.7 %all_gather.9 = bf16[2048,192]{0,1:T(8,128)(2,1)S(1)} all-gather(bf16[256,192]{0,1:T(8,128)(2,1)S(1)} %convolution_convert_fusion.3), channel_id=1, replica_groups=mesh['interval'=8,'seq'=8,'head'=8] {'seq'}, dimensions={0}, use_global_device_ids=true | all-gather | bytes 884736 | tf_op jit(solution)/shard_map/all_gather | solution.py:49
  23.5 0.4 convolution_convert_fusion.2
  23.9 0.4 convolution_convert_fusion.1
  24.3 13.7 %all_gather.10 = bf16[2048,192]{1,0:T(8,128)(2,1)S(1)} all-gather(bf16[256,192]{1,0:T(8,128)(2,1)S(1)} %convolution_convert_fusion.1), channel_id=1, replica_groups=mesh['interval'=8,'seq'=8,'head'=8] {'seq'}, dimensions={0}, use_global_device_ids=true | all-gather | bytes 884736 | tf_op jit(solution)/shard_map/all_gather | solution.py:50
  38.1 0.5 fusion.31
  38.6 0.4 fusion.4
  39.1 0.7 multiply_reduce_fusion
  39.8 0.6 multiply_convert_fusion
  40.4 1.0 copy-done.1
  41.4 1.3 fusion.2
  42.7 0.0 reduce-scatter.5.cloned.1.call-update
  42.7 0.0 copy-start.13
  42.7 0.0 copy-start.14
  42.7 0.0 reduce-scatter.7.cloned.1.call-start
  42.8 2.4 convolution_convert_fusion
  45.2 0.0 reduce-scatter.7.cloned.1.call-update
  45.3 0.0 reduce-scatter.9.cloned.1.call-start
  45.3 0.1 add.138
  45.4 0.1 add.139
  45.5 0.1 squeeze.15
  45.6 0.1 reshape.274
  45.6 0.1 squeeze.16
  45.7 0.1 compare_select_fusion
  45.8 0.1 reshape.282
  45.9 0.1 lt.65
  46.0 0.1 lt.67
  46.1 0.1 lt.68
  46.2 1.4 convolution_convert_fusion.4
  47.5 0.6 gather_fusion
  48.2 14.2 %all_gather.11 = bf16[2048,128]{1,0:T(8,128)(2,1)} all-gather(bf16[256,128]{1,0:T(8,128)(2,1)S(1)} %convolution_convert_fusion.4), channel_id=1, replica_groups=mesh['interval'=8,'seq'=8,'head'=8] {'seq'}, dimensions={0}, use_global_device_ids=true | all-gather | bytes 589824 | tf_op jit(solution)/shard_map/all_gather | solution.py:51
  62.4 1.7 gather_fusion.1
  64.1 0.1 fusion.23
  64.2 0.0 copy-start.12
  64.2 1.9 scatter_custom_fusion
  66.2 2.1 convert_element_type.105
  68.2 0.0 reduce-scatter.9.cloned.1.call-update
  68.3 0.0 all-reduce.5.cloned.1.call-start
  68.3 0.5 fusion.6
  68.8 0.0 copy-start.8
  68.9 0.6 copy-done.8
  69.5 1.3 fusion.12
  70.8 12.8 %reduce-scatter.5.cloned.1.call-done = bf16[256,192]{0,1:T(8,128)(2,1)} async-done(((bf16[2048,192]{0,1:T(8,128)(2,1)}), bf16[256,192]{0,1:T(8,128)(2,1)}) %reduce-scatter.5.cloned.1.call-update) | async-done | bytes 98320 | tf_op jit(solution)/shard_map/reduce_scatter | solution.py:85
  83.6 2.3 fusion.10
  85.9 36.5 %reduce-scatter.7.cloned.1.call-done = bf16[256,192]{0,1:T(8,128)(2,1)} async-done(((bf16[2048,192]{0,1:T(8,128)(2,1)}), bf16[256,192]{0,1:T(8,128)(2,1)}) %reduce-scatter.7.cloned.1.call-update) | async-done | bytes 98320 | tf_op jit(solution)/shard_map/reduce_scatter | solution.py:88
  122.4 2.2 fusion.8
  124.6 0.0 all-reduce.5.cloned.1.call-update
  124.6 0.0 reduce-scatter.11.cloned.1.call-start
  124.7 0.1 reshape_squeeze.4
  124.8 0.5 fusion.28
  125.3 1.3 fusion.32
  126.6 34.3 %reduce-scatter.9.cloned.1.call-done = bf16[256,128]{1,0:T(8,128)(2,1)} async-done(((bf16[2048,128]{1,0:T(8,128)(2,1)}), bf16[256,128]{1,0:T(8,128)(2,1)}) %reduce-scatter.9.cloned.1.call-update) | async-done | bytes 65552 | tf_op jit(solution)/shard_map/reduce_scatter | solution.py:120
  161.0 0.8 convert_element_type.106
  161.8 1.2 scatter_custom_fusion.1
  163.0 1.3 convolution_add_fusion.2
  164.4 1.6 convolution_add_fusion.1
  166.0 1.2 fusion
  167.3 0.0 reduce-scatter.11.cloned.1.call-update
  167.3 98.1 %all-reduce.5.cloned.1.call-done = (f32[192,1536]{1,0:T(8,128)}, f32[192,1536]{1,0:T(8,128)}, f32[192,1536]{1,0:T(8,128)}) async-done(((f32[192,1536]{1,0:T(8,128)}, f32[192,1536]{1,0:T(8,128)}, f32[192,1536]{1,0:T(8,128)}), (f32[192,1536]{1,0:T(8,128)}, f32[192,1536]{1,0:T(8,128)}, f32[192,1536]{1,0:T(8,128)})) %all-reduce.5.cloned.1.call-update) | async-done | bytes 3538960 | tf_op jit(solution)/shard_map/psum | solution.py:12
  265.4 58.6 %all-reduce.6 = (bf16[192,1536]{1,0:T(8,128)(2,1)}, bf16[192,1536]{1,0:T(8,128)(2,1)}, bf16[192,1536]{1,0:T(8,128)(2,1)}) all-reduce(f32[192,1536]{1,0:T(8,128)} %get-tuple-element.7, f32[192,1536]{1,0:T(8,128)} %get-tuple-element.8, f32[192,1536]{1,0:T(8,128)} %get-tuple-element.9), channel_id=1, replica_groups=mesh['interval'=8,'seq'=8,'head'=8] {'seq'}, use_global_device_ids=true, to_apply=%region_11.12 | all-reduce | flops 884736 | bytes 5308416 | tf_op jit(solution)/shard_map/psum | solution.py:13
  (32 shorter events, 0.1 us)
Async XLA Ops:
  7.2 1.1 copy-start
  7.2 16.3 %copy-start.5 = (bf16[192,1536]{1,0:T(8,128)(2,1)S(1)}, bf16[192,1536]{1,0:T(8,128)(2,1)}, u32[]{:S(2)}) copy-start(bf16[192,1536]{1,0:T(8,128)(2,1)} %param.12) | copy-start | bytes 1769476
  7.2 16.7 %copy-start.9 = (bf16[192,1536]{1,0:T(8,128)(2,1)S(1)}, bf16[192,1536]{1,0:T(8,128)(2,1)}, u32[]{:S(2)}) copy-start(bf16[192,1536]{1,0:T(8,128)(2,1)} %param.14) | copy-start | bytes 1769476
  7.2 76.4 %reduce-scatter.5.cloned.1.call-start = ((), (), s32[]{:S(2)}) async-start(), calls=%async_computation.4 | async-start | bytes 884736 | tf_op jit(solution)/shard_map/reduce_scatter | solution.py:85
  23.5 14.5 %copy-start.3 = (bf16[2048,192]{0,1:T(8,128)(2,1)}, bf16[2048,192]{0,1:T(8,128)(2,1)S(1)}, u32[]{:S(2)}) copy-start(bf16[2048,192]{0,1:T(8,128)(2,1)S(1)} %all_gather.9) | copy-start | bytes 2359300
  38.1 1.0 copy-start.15
  40.4 1.0 copy-start.1
  42.7 2.8 copy-start.10
  42.7 2.8 copy-start.11
  42.7 2.9 copy-start.13
  42.7 3.3 copy-start.14
  42.7 79.6 %reduce-scatter.7.cloned.1.call-start = ((), (), s32[]{:S(2)}) async-start(), calls=%async_computation.5 | async-start | bytes 884736 | tf_op jit(solution)/shard_map/reduce_scatter | solution.py:88
  45.3 115.7 %reduce-scatter.9.cloned.1.call-start = ((), (), s32[]{:S(2)}) async-start(), calls=%async_computation.6 | async-start | bytes 589824 | tf_op jit(solution)/shard_map/reduce_scatter | solution.py:120
  47.5 20.8 %copy-start.2 = (bf16[256,2048]{1,0:T(8,128)(2,1)S(1)}, bf16[256,2048]{1,0:T(8,128)(2,1)}, u32[]{:S(2)}) copy-start(bf16[256,2048]{1,0:T(8,128)(2,1)} %copy-done.1) | copy-start | bytes 3145732
  47.5 20.8 %copy-start.4 = (bf16[2048,192]{0,1:T(8,128)(2,1)S(1)}, bf16[2048,192]{0,1:T(8,128)(2,1)}, u32[]{:S(2)}) copy-start(bf16[2048,192]{0,1:T(8,128)(2,1)} %copy-done.3) | copy-start | bytes 2359300
  64.2 4.6 %copy-start.12 = (f32[64]{0:T(128)}, f32[64]{0:T(128)S(1)}, u32[]{:S(2)}) copy-start(f32[64]{0:T(128)S(1)} %fusion.29) | copy-start | bytes 772
  68.3 197.2 %all-reduce.5.cloned.1.call-start = ((), (), s32[]{:S(2)}) async-start(), calls=%async_computation.8 | async-start | bytes 7077888 | tf_op jit(solution)/shard_map/psum | solution.py:12
  68.8 0.6 copy-start.8
  124.6 38.4 %copy-start.6 = (bf16[192,1536]{1,0:T(8,128)(2,1)S(1)}, bf16[192,1536]{1,0:T(8,128)(2,1)}, u32[]{:S(2)}) copy-start(bf16[192,1536]{1,0:T(8,128)(2,1)} %param.13) | copy-start | bytes 1769476
  124.6 199.3 %reduce-scatter.11.cloned.1.call-start = ((), (), s32[]{:S(2)}) async-start(), calls=%async_computation.7 | async-start | bytes 884736 | tf_op jit(solution)/shard_map/reduce_scatter | solution.py:134
  164.4 1.6 copy-start.7
Sparse Core Ops, SparseCore 0:
  42.8 40.7 reduce-scatter.4
  86.7 35.6 reduce-scatter.6
  125.7 35.1 reduce-scatter.8
  163.6 101.8 all-reduce.4
  268.7 40.4 reduce-scatter.10
